TPU v7x, 256 devices: a whole 4x4x8 slice. The times are simulated.
256 devices in a mesh: member: 2 (over x_lo), space: 128 (over z, y, x_hi, core).
Axes of the slice: x: 4 (x_hi: 2, x_lo: 2; x = x_hi * 2 + x_lo), y: 4, z: 8, core: 2. Of those that a mesh axis runs over, the one named last changes fastest.
Arguments:
- params: float32 [256, 512, 1024], P('member', 'space'), may hold values from -2 to 2
- state: float32 [256, 512, 1024], P('member', 'space'), may hold values from -6 to 6
- regime: int32 [512, 1024], P('space'), may hold values from 0 to 7
- regime_coefs: float32 [8, 4], replicated, may hold values from 0.1 to 0.5
- observation_index: int32 [65536], P('space'), may hold values from 0 to 524287, as said below
- measured_values: float32 [65536], P('space'), may hold values from -6 to 6
- observation_spread: float32 [65536], P('space'), may hold values from 0.1 to 1
- observation_jitter: float32 [256, 65536], P('member', 'space'), may hold values from -6 to 6
Outputs:
- revised_log_diffusivity: float32 [256, 512, 1024], P('member', 'space')
- predicted_member_state: float32 [256, 512, 1024], P('member', 'space')
Inputs may be any that keep to these rules, and one draw needn't show every extreme that they name: `observation_index`: observation o lies in the strip of rows o // 512 * 4 up to (o // 512 + 1) * 4 - 1; the first observation of each strip sits on its first cell, the second on its last cell; cells may repeat.
All inputs are finite; a program needn't handle non-finite values.
Results may differ from a plain program's by a relative error of at most 0.015.
Values sent between devices are 32-bit elements; how exact they have to be, the bound alone decides.
No kernel may reach another device: no remote copies, remote signals or barrier semaphores. Data moves between devices by JAX's collectives and lax.ppermute only.
A program may use at most 64 MiB of HBM per device.

v0:
```python
import math
import jax
import jax.numpy as jnp
from jax import lax
from jax.sharding import PartitionSpec as P

time_step = 0.06


def with_halo(cells, sides, width):
    for axis, dim in sides:
        count = lax.axis_size(axis)
        ends = count - 1
        head = lax.slice_in_dim(cells, 0, width, axis=dim)
        tail = lax.slice_in_dim(cells, cells.shape[dim] - width, cells.shape[dim], axis=dim)
        cells = jnp.concatenate(
            [
                lax.ppermute(tail, axis, [(i, (i + 1) % count) for i in range(ends)]),
                cells,
                lax.ppermute(head, axis, [((i + 1) % count, i) for i in range(ends)]),
            ],
            axis=dim,
        )
    return cells


def coef_fields(regime, regime_coefs):
    levels = jnp.arange(regime_coefs.shape[0], dtype=jnp.int32)
    onehot = (regime[None, :, :] == levels[:, None, None]).astype(jnp.float32)
    return jnp.einsum("rd,rxy->dxy", regime_coefs, onehot, precision=lax.Precision.HIGHEST)


def advance(extended, rates, coefs):
    center = extended[..., 1:-1, :]
    widths = [(0, 0)] * (center.ndim - 1) + [(1, 1)]
    padded_cols = jnp.pad(center, widths)
    above = extended[..., :-2, :]
    below = extended[..., 2:, :]
    left_side = padded_cols[..., :-2]
    right_side = padded_cols[..., 2:]
    flow = coefs[0] * (above - center) + coefs[1] * (below - center)
    flow = flow + coefs[2] * (left_side - center) + coefs[3] * (right_side - center)
    return center + rates * flow


def body(
    params,
    state,
    regime,
    regime_coefs,
    observation_index,
    measured_values,
    observation_spread,
    observation_jitter,
):
    block_members = params.shape[0]
    strip_rows = params.shape[1]
    columns = params.shape[2]
    member_list = block_members * lax.axis_size("member")
    square_root_scale = math.sqrt(member_list - 1)
    coefs = coef_fields(regime, regime_coefs)
    rates = time_step * jnp.exp(params)
    current = state
    for repeat in range(2):
        extended = with_halo(current, (("space", 1),), 1)
        current = advance(extended, rates, coefs)
    param_anom = params / square_root_scale
    slab_local_index = observation_index - lax.axis_index("space") * (strip_rows * columns)
    flattened_grid = current.reshape(block_members, strip_rows * columns)
    local_predictions = jnp.take(flattened_grid, slab_local_index, axis=1)
    predicted_fields, noise_draws = (
        lax.all_gather(local_predictions, "member", axis=0, tiled=True),
        lax.all_gather(observation_jitter, "member", axis=0, tiled=True),
    )
    ensemble_mean_prediction = jnp.sum(predicted_fields, axis=0) / member_list
    member_departures = (predicted_fields - ensemble_mean_prediction[None, :]) / (
        observation_spread[None, :] * square_root_scale
    )
    observation_misfits = (
        measured_values[None, :] + observation_spread[None, :] * noise_draws - predicted_fields
    ) / observation_spread[None, :]
    stacked = jnp.concatenate([member_departures, observation_misfits], axis=0)
    own_start = lax.axis_index("member") * block_members
    own_anoms = lax.dynamic_slice_in_dim(member_departures, own_start, block_members, 0)
    block_rows = jnp.dot(
        own_anoms, stacked.T, precision=lax.Precision.HIGHEST, preferred_element_type=jnp.float32
    )
    block_rows = lax.psum(block_rows, "space")
    gram_full = lax.all_gather(block_rows, "member", axis=0, tiled=True)
    gram = gram_full[:, :member_list]
    cross = gram_full[:, member_list:]
    system = jnp.eye(member_list, dtype=jnp.float32) + gram
    factor = jnp.linalg.cholesky(system)
    mixing = jax.scipy.linalg.cho_solve((factor, True), cross)
    empty = jnp.zeros(params.shape, jnp.float32)
    piece = lax.all_gather(param_anom, "member", axis=0, tiled=True)
    weights = lax.dynamic_slice(mixing, (0, own_start), (piece.shape[0], block_members))
    update = empty + jnp.einsum("kj,kxy->jxy", weights, piece, precision=lax.Precision.HIGHEST)
    revised_log_diffusivity = params + update
    return (revised_log_diffusivity, current)


def solution(mesh):
    in_specs = (
        P("member", "space", None),
        P("member", "space", None),
        P("space", None),
        P(),
        P("space"),
        P("space"),
        P("space"),
        P("member", "space"),
    )
    out_specs = (P("member", "space", None), P("member", "space", None))
    return jax.shard_map(body, mesh=mesh, in_specs=in_specs, out_specs=out_specs, check_vma=False)
```

profile of v0, /device:TPU:2, one launch (start us, length us, event | category | flops | bytes accessed | tf_op | source)
XLA Modules:
  0.0 1354.0 jit_solution(15341635839725576717)
XLA Ops:
  8.0 0.0 copy-start
  8.0 0.0 all-reduce.5.cloned.1.call-start
  8.1 0.0 copy-start.5
  8.1 2.8 copy.28
  10.9 0.0 copy-start.3
  10.9 1.3 copy-done.3
  12.2 1.0 fusion.53
  13.2 1.8 collective-permute-start
  15.0 1.3 collective-permute-start.1
  16.3 0.0 copy-done
  16.3 0.0 copy-done.5
  16.3 0.2 convolution_bitcast_fusion
  16.6 0.1 collective-permute-done
  16.7 4.2 collective-permute-done.1
  20.9 0.0 copy-done.1
  20.9 5.7 fusion.5
  26.6 0.0 copy-start.2
  26.6 1.3 copy-done.2
  28.0 1.1 fusion.52
  29.0 13.7 %collective-permute-start.2 = (f32[128,1,1024]{2,0,1:T(8,128)}, f32[128,1,1024]{2,0,1:T(8,128)}, u32[]{:S(2)}, u32[]{:S(2)}) collective-permute-start(f32[128,1,1024]{2,0,1:T(8,128)} %get-tuple-element.28), channel_id=1, source_target_pairs={{0,1},{1,2},{2,3},{3,4},{4,5},{5,6},{6,7},{7,8},{8,9},{9,10},{10,1... | collective-permute-start | bytes 1572872 | tf_op jit(solution)/shard_map/ppermute | solution.py:18
  42.7 1.3 collective-permute-start.3
  44.1 0.1 copy.30
  44.2 15.5 %all_gather.13 = f32[256,512]{0,1:T(8,128)S(1)} all-gather(f32[128,512]{0,1:T(8,128)S(1)} %copy.30), channel_id=1, replica_groups=mesh['member'=2,'space'=128] {'member'}, dimensions={0}, use_global_device_ids=true | all-gather | bytes 786432 | tf_op jit(solution)/shard_map/all_gather | solution.py:73
  59.7 0.0 collective-permute-done.2
  59.7 0.0 collective-permute-done.3
  59.7 7.4 fusion.13
  67.1 2.9 copy.29
  70.0 2.6 gather_fusion
  72.6 0.1 select_bitcast_fusion
  72.8 9.4 all_gather.12
  82.2 0.1 reduce_sum.9
  82.3 0.0 copy-done.8
  82.3 0.3 subtract_divide_fusion.1
  82.7 2.5 fusion.26
  85.2 0.0 all-reduce.5.cloned.1.call-update
  85.3 0.0 all-gather.2.cloned.1.call-start
  85.3 0.5 all-gather.2.cloned.1.call-update
  85.9 4.3 copy.37
  90.1 1177.7 %all-reduce.5.cloned.1.call-done = f32[128,512]{0,1:T(8,128)} async-done(((f32[128,512]{0,1:T(8,128)}), f32[128,512]{0,1:T(8,128)}) %all-reduce.5.cloned.1.call-update) | async-done | bytes 262160 | tf_op jit(solution)/shard_map/psum | solution.py:88
  1267.8 8.1 all_gather.14
  1276.0 0.1 copy.32
  1276.2 11.7 cholesky.50
  1287.9 9.8 custom-call.18
  1297.7 0.2 constant_dynamic-update-slice_fusion
  1298.0 0.3 convolution_subtract_fusion.2
  1298.2 11.7 cholesky.105
  1310.0 0.6 compare_reduce_fusion
  1310.6 0.6 compare_reduce_fusion.1
  1312.5 0.1 triangular_solve.69
  1312.6 4.0 while.1
  1312.7 0.6 fusion.64
  1313.3 1.3 bitcast_dynamic-update-slice_fusion.2
  1314.7 0.6 fusion.64
  1315.2 1.3 bitcast_dynamic-update-slice_fusion.2
  1316.6 19.7 %custom-call.19 = f32[2,128,128]{1,2,0:T(8,128)S(1)} custom-call(f32[2,128,128]{2,1,0:T(8,128)S(1)} %get-tuple-element.9), custom_call_target="InvertDiagBlocksLowerTriangular" | custom-call | tf_op jit(solution)/shard_map/jit(_cho_solve)/triangular_solve | solution.py:94
  1336.2 0.3 fusion.35
  1336.6 0.4 convolution_subtract_fusion.1
  1337.0 0.3 fusion.43
  1337.3 0.3 fusion.42
  1337.5 0.3 convolution_subtract_fusion
  1337.9 0.3 fusion.41
  1338.1 0.0 all-gather.2.cloned.1.call-done
  1338.2 5.7 copy_add_fusion
  1343.9 2.7 copy.36
  (26 shorter events, 0.3 us)
Async XLA Ops:
  8.0 8.3 copy-start
  8.0 1259.8 %all-reduce.5.cloned.1.call-start = ((), (), s32[]{:S(2)}) async-start(), calls=%async_computation | async-start | bytes 524288 | tf_op jit(solution)/shard_map/psum | solution.py:88
  8.1 8.3 copy-start.5
  10.9 1.3 copy-start.3
  12.2 8.7 copy-start.1
  13.2 3.5 collective-permute-start
  15.0 5.9 collective-permute-start.1
  26.6 1.3 copy-start.2
  28.0 16.1 %copy-start.7 = (s32[512]{0:T(512)S(1)}, s32[512]{0:T(512)}, u32[]{:S(2)}) copy-start(s32[512]{0:T(512)} %param.12) | copy-start | bytes 6148
  28.0 16.1 %copy-start.4 = (f32[128,512]{1,0:T(8,128)S(1)}, f32[128,512]{1,0:T(8,128)}, u32[]{:S(2)}) copy-start(f32[128,512]{1,0:T(8,128)} %param.15) | copy-start | bytes 786436
  28.0 31.7 %copy-start.6 = (f32[512]{0:T(512)S(1)}, f32[512]{0:T(512)}, u32[]{:S(2)}) copy-start(f32[512]{0:T(512)} %param.14) | copy-start | bytes 6148
  29.0 30.6 %collective-permute-start.2 = (f32[128,1,1024]{2,0,1:T(8,128)}, f32[128,1,1024]{2,0,1:T(8,128)}, u32[]{:S(2)}, u32[]{:S(2)}) collective-permute-start(f32[128,1,1024]{2,0,1:T(8,128)} %get-tuple-element.28), channel_id=1, source_target_pairs={{0,1},{1,2},{2,3},{3,4},{4,5},{5,6},{6,7},{7,8},{8,9},{9,10},{10,1... | collective-permute-start | bytes 1572872 | tf_op jit(solution)/shard_map/ppermute | solution.py:18
  42.7 16.9 %collective-permute-start.3 = (f32[128,1,1024]{2,0,1:T(8,128)}, f32[128,1,1024]{2,0,1:T(8,128)}, u32[]{:S(2)}, u32[]{:S(2)}) collective-permute-start(f32[128,1,1024]{2,0,1:T(8,128)} %get-tuple-element.29), channel_id=1, source_target_pairs={{1,0},{2,1},{3,2},{4,3},{5,4},{6,5},{7,6},{8,7},{9,8},{10,9},{11,1... | collective-permute-start | bytes 1572872 | tf_op jit(solution)/shard_map/ppermute | solution.py:20
  70.0 12.3 copy-start.8
  85.3 1252.9 %all-gather.2.cloned.1.call-start = ((), (), s32[]{:S(2)}) async-start(), calls=%async_computation.1 | async-start | bytes 6291456 | tf_op jit(solution)/shard_map/all_gather | solution.py:96
Sparse Core Ops, SparseCore 0:
  85.4 1182.4 all-reduce.4
Sparse Core Ops, SparseCore 1:
  87.5 65.5 all-gather.1
where the time goes:
time: 1350 us
  waiting for transfers between devices  1180 us (87%)
  other arithmetic  68.1 us (5%)
  blocking collectives  32.9 us (2%)
  local copies, waits for them, and re-layouts  24.2 us (2%)
  starting transfers between devices  18.1 us (1%)
  between operations  17.1 us (1%)
    psum x1, waiting for transfers between devices, body(): block_rows = lax.psum(block_rows, 'space')  1180 us
    another operation x7, other arithmetic, body(): factor = jnp.linalg.cholesky(system)  34.6 us
  transfers between devices with their start and end apart: 6, of which 3 were waited for; matrix products, arithmetic and copies ran while one was open for 5% of the time, Pallas kernels for 0%

commit v1 on v0

--- a/solution.py
+++ b/solution.py
@@ -85,7 +85,7 @@
     block_rows = jnp.dot(
         own_anoms, stacked.T, precision=lax.Precision.HIGHEST, preferred_element_type=jnp.float32
     )
-    block_rows = lax.psum(block_rows, "space")
+    block_rows = jnp.sum(lax.all_gather(block_rows, "space"), axis=0)
     gram_full = lax.all_gather(block_rows, "member", axis=0, tiled=True)
     gram = gram_full[:, :member_list]
     cross = gram_full[:, member_list:]

time: 1350 us -> 406 us (0.30)
  waiting for transfers between devices: 1180 us -> 216 us
    psum x1 -> x0, waiting for transfers between devices: 1180 us -> none  [body(): block_rows = lax.psum(block_rows, 'space')]
    all_gather x0 -> x1, waiting for transfers between devices: none -> 211 us  [body(): block_rows = jnp.sum(lax.all_gather(block_rows, 'space'), axis=0)]
  transfers between devices with their start and end apart: 6 -> 6, of which waited for: 3 -> 3; matrix products, arithmetic and copies ran while one was open for 5% -> 19% of each run, Pallas kernels for 0% -> 0%
where the time goes in v1:
time: 406 us; the launch traced here: 404 us
  waiting for transfers between devices  216 us (53%)
  other arithmetic  80.3 us (20%)
  blocking collectives  40.2 us (10%)
  local copies, waits for them, and re-layouts  24.3 us (6%)
  starting transfers between devices  18.1 us (4%)
  between operations  15.6 us (4%)
  matrix products  9.79 us (2%)
    all_gather x1, waiting for transfers between devices, body(): block_rows = jnp.sum(lax.all_gather(block_rows, 'space'), axis=0)  211 us
    another operation x7, other arithmetic, body(): factor = jnp.linalg.cholesky(system)  34.6 us
    another operation x3, other arithmetic, body(): mixing = jax.scipy.linalg.cho_solve((factor, True), cross)  19.7 us
    all_gather x1, blocking collectives, body(): lax.all_gather(observation_jitter, 'member', axis=0, tiled=True)  15.5 us
    ppermute x2, starting transfers between devices, with_halo(): lax.ppermute(tail, axis, [(i, (i + 1) % count) for i in range(ends)])  15.5 us
    all_gather x1, blocking collectives, body(): gram_full = lax.all_gather(block_rows, 'member', axis=0, tiled=True)  15.4 us
    add x2, other arithmetic, advance(): return center + rates * flow  13 us
    unnamed x26, local copies, waits for them, and re-layouts  12.6 us
  transfers between devices with their start and end apart: 6, of which 3 were waited for; matrix products, arithmetic and copies ran while one was open for 19% of the time, Pallas kernels for 0%

profile of v1, /device:TPU:2, one launch (start us, length us, event | category | flops | bytes accessed | tf_op | source)
XLA Modules:
  0.0 404.2 jit_solution(10693556592101273321)
XLA Ops:
  7.2 0.0 copy-start
  7.2 0.0 all-gather.6.cloned.1.call-start
  7.2 2.8 copy.27
  10.1 0.0 copy-start.4
  10.1 1.3 copy-done.4
  11.4 1.0 fusion.53
  12.4 1.8 collective-permute-start
  14.2 1.3 collective-permute-start.1
  15.5 0.2 convolution_bitcast_fusion
  15.8 0.1 collective-permute-done
  15.9 4.2 %collective-permute-done.1 = f32[128,1,1024]{2,0,1:T(8,128)S(1)} collective-permute-done((f32[128,1,1024]{2,0,1:T(8,128)}, f32[128,1,1024]{2,0,1:T(8,128)S(1)}, u32[]{:S(2)}, u32[]{:S(2)}) %collective-permute-start.1) | collective-permute-done | bytes 524320 | tf_op jit(solution)/shard_map/ppermute | solution.py:20
  20.1 5.7 %fusion.5 = f32[128,4,1024]{2,0,1:T(8,128)S(1)} fusion(f32[128,4,1024]{2,0,1:T(8,128)} %copy-done.4, f32[128,1,1024]{2,0,1:T(8,128)S(1)} %collective-permute-done.1, f32[128,1,1024]{2,0,1:T(8,128)S(1)} %collective-permute-done, f32[128,4,1024]{2,1,0:T(4,128)S(1)} %copy-done.2, f32[4,1024]{1,0:T(4,128)S(1)} %get-tuple-element.44, ...), kind=kLoop, calls=%fused_computation.12 | loop fusion | flops 8388608 | bytes 7405568 | tf_op jit(solution)/shard_map/add | solution.py:43
  25.8 0.0 copy-start.3
  25.8 1.3 copy-done.3
  27.2 1.1 fusion.52
  28.2 13.7 %collective-permute-start.2 = (f32[128,1,1024]{2,0,1:T(8,128)}, f32[128,1,1024]{2,0,1:T(8,128)}, u32[]{:S(2)}, u32[]{:S(2)}) collective-permute-start(f32[128,1,1024]{2,0,1:T(8,128)} %get-tuple-element.28), channel_id=1, source_target_pairs={{0,1},{1,2},{2,3},{3,4},{4,5},{5,6},{6,7},{7,8},{8,9},{9,10},{10,1... | collective-permute-start | bytes 1572872 | tf_op jit(solution)/shard_map/ppermute | solution.py:18
  41.9 1.3 collective-permute-start.3
  43.2 0.1 copy.29
  43.4 15.5 %all_gather.19 = f32[256,512]{0,1:T(8,128)S(1)} all-gather(f32[128,512]{0,1:T(8,128)S(1)} %copy.29), channel_id=1, replica_groups=mesh['member'=2,'space'=128] {'member'}, dimensions={0}, use_global_device_ids=true | all-gather | bytes 786432 | tf_op jit(solution)/shard_map/all_gather | solution.py:73
  58.9 0.0 collective-permute-done.2
  58.9 0.0 collective-permute-done.3
  58.9 7.3 %fusion.13 = (f32[128,4,1024]{2,0,1:T(8,128)}, f32[128,4,1024]{2,0,1:T(8,128)}) fusion(f32[128,4,1024]{2,0,1:T(8,128)} %copy-done.3, f32[128,1,1024]{2,0,1:T(8,128)} %collective-permute-done.3, f32[128,1,1024]{2,0,1:T(8,128)} %collective-permute-done.2, f32[128,4,1024]{2,1,0:T(4,128)S(1)} %copy-done.2, f32[4,1024]{1,0:T(4,128)S(1)} %get-tuple-element.44, ...), kind=kLoop, calls=%fused_computation.20 | loop fusion | flops 8912896 | bytes 9502720 | tf_op jit(solution)/shard_map/add | solution.py:43
  66.1 2.9 copy.28
  69.0 2.6 gather_fusion
  71.7 0.1 select_bitcast_fusion
  71.8 9.4 %all_gather.18 = f32[256,512]{0,1:T(8,128)S(1)} all-gather(f32[128,512]{0,1:T(8,128)S(1)} %select_bitcast_fusion), channel_id=1, replica_groups=mesh['member'=2,'space'=128] {'member'}, dimensions={0}, use_global_device_ids=true | all-gather | bytes 786432 | tf_op jit(solution)/shard_map/all_gather | solution.py:72
  81.2 0.1 reduce_sum.18
  81.4 0.0 copy-done.9
  81.4 0.3 subtract_divide_fusion.1
  81.7 1.5 fusion.26
  83.3 0.0 all-gather.6.cloned.1.call-update
  83.3 0.0 all-gather.4.cloned.1.call-start
  83.4 0.7 all-gather.4.cloned.1.call-update
  84.1 4.3 %copy.36 = f32[128,4,1024]{2,1,0:T(4,128)} copy(f32[128,4,1024]{2,0,1:T(8,128)} %get-tuple-element.26) | data formatting | bytes 4194304
  88.3 210.5 %all-gather.6.cloned.1.call-done = f32[16384,512]{1,0:T(8,128)} async-done(((f32[128,512]{1,0:T(8,128)}), f32[16384,512]{1,0:T(8,128)}) %all-gather.6.cloned.1.call-update) | async-done | bytes 33554448 | tf_op jit(solution)/shard_map/all_gather | solution.py:88
  298.8 12.3 %reduce_sum.19 = f32[128,512]{1,0:T(8,128)S(1)} reduce(f32[128,128,512]{2,1,0:T(8,128)} %bitcast.57, f32[]{:T(128)} %constant.118.clone.1), dimensions={0}, to_apply=%region_1.2 | reduce | flops 8323072 | bytes 33816580 | tf_op jit(solution)/shard_map/reduce_sum | solution.py:88
  311.2 0.1 copy.30
  311.3 15.4 %all_gather.22 = f32[256,512]{0,1:T(8,128)S(1)} all-gather(f32[128,512]{0,1:T(8,128)S(1)} %copy.30), channel_id=1, replica_groups=mesh['member'=2,'space'=128] {'member'}, dimensions={0}, use_global_device_ids=true | all-gather | bytes 786432 | tf_op jit(solution)/shard_map/all_gather | solution.py:89
  326.7 0.1 copy.31
  326.9 11.7 %cholesky.50 = f32[128,128]{1,0:T(8,128)S(1)} custom-call(f32[128,128]{1,0:T(8,128)S(1)} %cholesky.118), custom_call_target="Cholesky" | custom-call | tf_op jit(solution)/shard_map/jit(cholesky)/cholesky | solution.py:93
  338.7 9.8 %custom-call.18 = f32[1,128,128]{1,2,0:T(8,128)S(1)} custom-call(f32[1,128,128]{2,1,0:T(8,128)S(1)} %get-tuple-element.37), custom_call_target="InvertDiagBlocksLowerTriangular" | custom-call | tf_op jit(solution)/shard_map/jit(cholesky)/cholesky | solution.py:93
  348.5 0.2 constant_dynamic-update-slice_fusion
  348.7 0.3 convolution_subtract_fusion.2
  348.9 11.7 %cholesky.105 = f32[128,128]{1,0:T(8,128)S(1)} custom-call(f32[128,128]{1,0:T(8,128)S(1)} %convolution_subtract_fusion.2), custom_call_target="Cholesky" | custom-call | tf_op jit(solution)/shard_map/jit(cholesky)/cholesky | solution.py:93
  360.7 0.6 compare_reduce_fusion
  361.3 0.6 compare_reduce_fusion.1
  363.2 0.1 triangular_solve.69
  363.3 4.0 while.1
  363.5 0.6 fusion.64
  364.1 1.3 bitcast_dynamic-update-slice_fusion.2
  365.4 0.6 fusion.64
  366.0 1.3 bitcast_dynamic-update-slice_fusion.2
  367.3 19.7 %custom-call.19 = f32[2,128,128]{1,2,0:T(8,128)S(1)} custom-call(f32[2,128,128]{2,1,0:T(8,128)S(1)} %get-tuple-element.9), custom_call_target="InvertDiagBlocksLowerTriangular" | custom-call | tf_op jit(solution)/shard_map/jit(_cho_solve)/triangular_solve | solution.py:94
  387.0 0.3 fusion.35
  387.3 0.4 convolution_subtract_fusion.1
  387.7 0.3 fusion.43
  388.0 0.3 fusion.42
  388.3 0.3 convolution_subtract_fusion
  388.6 0.3 fusion.41
  388.9 0.0 all-gather.4.cloned.1.call-done
  388.9 0.0 copy-start.1
  388.9 5.7 %copy_add_fusion = f32[128,4,1024]{2,0,1:T(8,128)S(1)} fusion(f32[128,4,1024]{2,1,0:T(4,128)S(1)} %copy-done.2, f32[256,4,1024]{2,0,1:T(8,128)} %all-gather.4.cloned.1.call-done, s32[]{:T(128)S(6)} %select_n.19, f32[128,256]{1,0:T(8,128)S(1)} %fusion.41, f32[128,256]{1,0:T(8,128)S(1)} %fusion.42), kind=kOutput, calls=%fused_computation.39 | convolution fusion | flops 1611169792 | bytes 8650756 | tf_op jit(solution)/shard_map/kj,kxy->jxy/dot_general | solution.py:98
  394.6 2.7 copy.35
  397.3 0.0 copy-done.1
  (30 shorter events, 0.3 us)
Async XLA Ops:
  7.2 8.3 %copy-start = (f32[8,4]{0,1:T(4,128)S(1)}, f32[8,4]{0,1:T(4,128)}, u32[]{:S(2)}) copy-start(f32[8,4]{0,1:T(4,128)} %param.11) | copy-start | bytes 388
  7.2 291.7 %all-gather.6.cloned.1.call-start = ((), (), s32[]{:S(2)}) async-start(), calls=%async_computation.1 | async-start | bytes 33816576 | tf_op jit(solution)/shard_map/all_gather | solution.py:88
  7.2 8.3 %copy-start.6 = (s32[4,1024]{1,0:T(4,128)S(1)}, s32[4,1024]{1,0:T(4,128)}, u32[]{:S(2)}) copy-start(s32[4,1024]{1,0:T(4,128)} %param.10) | copy-start | bytes 49156
  10.1 1.3 copy-start.4
  11.4 8.7 %copy-start.2 = (f32[128,4,1024]{2,1,0:T(4,128)S(1)}, f32[128,4,1024]{2,1,0:T(4,128)}, u32[]{:S(2)}) copy-start(f32[128,4,1024]{2,1,0:T(4,128)} %param.8) | copy-start | bytes 6291460
  12.4 3.5 collective-permute-start
  14.2 5.9 %collective-permute-start.1 = (f32[128,1,1024]{2,0,1:T(8,128)}, f32[128,1,1024]{2,0,1:T(8,128)S(1)}, u32[]{:S(2)}, u32[]{:S(2)}) collective-permute-start(f32[128,1,1024]{2,0,1:T(8,128)} %get-tuple-element.31), channel_id=1, source_target_pairs={{1,0},{2,1},{3,2},{4,3},{5,4},{6,5},{7,6},{8,7},{9,8},{10,9},{11,1... | collective-permute-start | bytes 1572872 | tf_op jit(solution)/shard_map/ppermute | solution.py:20
  25.8 1.3 copy-start.3
  27.2 16.1 %copy-start.8 = (s32[512]{0:T(512)S(1)}, s32[512]{0:T(512)}, u32[]{:S(2)}) copy-start(s32[512]{0:T(512)} %param.12) | copy-start | bytes 6148
  27.2 16.1 %copy-start.5 = (f32[128,512]{1,0:T(8,128)S(1)}, f32[128,512]{1,0:T(8,128)}, u32[]{:S(2)}) copy-start(f32[128,512]{1,0:T(8,128)} %param.15) | copy-start | bytes 786436
  27.2 31.7 %copy-start.7 = (f32[512]{0:T(512)S(1)}, f32[512]{0:T(512)}, u32[]{:S(2)}) copy-start(f32[512]{0:T(512)} %param.14) | copy-start | bytes 6148
  28.2 30.6 %collective-permute-start.2 = (f32[128,1,1024]{2,0,1:T(8,128)}, f32[128,1,1024]{2,0,1:T(8,128)}, u32[]{:S(2)}, u32[]{:S(2)}) collective-permute-start(f32[128,1,1024]{2,0,1:T(8,128)} %get-tuple-element.28), channel_id=1, source_target_pairs={{0,1},{1,2},{2,3},{3,4},{4,5},{5,6},{6,7},{7,8},{8,9},{9,10},{10,1... | collective-permute-start | bytes 1572872 | tf_op jit(solution)/shard_map/ppermute | solution.py:18
  41.9 16.9 %collective-permute-start.3 = (f32[128,1,1024]{2,0,1:T(8,128)}, f32[128,1,1024]{2,0,1:T(8,128)}, u32[]{:S(2)}, u32[]{:S(2)}) collective-permute-start(f32[128,1,1024]{2,0,1:T(8,128)} %get-tuple-element.29), channel_id=1, source_target_pairs={{1,0},{2,1},{3,2},{4,3},{5,4},{6,5},{7,6},{8,7},{9,8},{10,9},{11,1... | collective-permute-start | bytes 1572872 | tf_op jit(solution)/shard_map/ppermute | solution.py:20
  69.0 12.3 %copy-start.9 = (f32[512]{0:T(512)S(1)}, f32[512]{0:T(512)}, u32[]{:S(2)}) copy-start(f32[512]{0:T(512)} %param.13) | copy-start | bytes 6148
  83.3 305.6 %all-gather.4.cloned.1.call-start = ((), (), s32[]{:S(2)}) async-start(), calls=%async_computation | async-start | bytes 6291456 | tf_op jit(solution)/shard_map/all_gather | solution.py:96
  388.9 8.4 %copy-start.1 = (f32[8,4]{0,1:T(4,128)S(1)}, f32[8,4]{0,1:T(4,128)}, u32[]{:S(2)}) copy-start(f32[8,4]{0,1:T(4,128)} %param.11) | copy-start | bytes 388
Sparse Core Ops, SparseCore 0:
  83.4 215.3 all-gather.5
  300.6 63.9 all-gather.3
